TPU v7x, 512 devices: a whole 4x4x16 slice. The times are simulated.
512 devices in a mesh: dp: 8 (over y, core), expert: 64 (over x, z).
Axes of the slice: x: 4, y: 4, z: 16, core: 2. Of those that a mesh axis runs over, the one named last changes fastest.
Arguments:
- layer_in: bfloat16 [2048, 4096], P('expert', 'dp'), may hold values from -6 to 6
- grad_out: bfloat16 [2048, 4096], P('expert', 'dp'), may hold values from -6 to 6
- gate_prob: float32 [2048, 8], P('expert'), may hold values from 0.05 to 0.6
- expert_ids: int32 [2048, 8], P('expert'), may hold values from 0 to 31, as said below
- replica_index: int32 [2048, 8], P('expert'), may hold values from 0 to 3, as said below
- slot_expert: int32 [64], replicated, may hold values from 0 to 31, as said below
- w_gate: bfloat16 [64, 4096, 1024], P('expert', None, 'dp')
- w_up: bfloat16 [64, 4096, 1024], P('expert', None, 'dp')
- w_down: bfloat16 [64, 1024, 4096], P('expert', 'dp')
Outputs:
- grad_in: bfloat16 [2048, 4096], P('expert', 'dp')
- grad_w_down: bfloat16 [64, 1024, 4096], P('expert', 'dp')
Inputs may be any that keep to these rules, and one draw needn't show every extreme that they name: `slot_expert`: every expert owns one run of consecutive slots, counted cyclically (slot 63 is followed by slot 0), of 1 to 4 slots; the runs cover all 64 slots. `expert_ids`: the 8 experts of one token are different. `replica_index`: each entry is below the number of slots of the expert of the same choice. Of the 32 tokens of one index of expert, at most 8 choices go to any one slot, and in every draw some slot receives exactly 8 from the tokens of every index of expert.
All inputs are finite; a program needn't handle non-finite values.
Results may differ from a plain program's by a relative error of at most 0.014.
Values may be sent and summed in bfloat16 or wider, within the bound.
No kernel may reach another device: no remote copies, remote signals or barrier semaphores. Data moves between devices by JAX's collectives and lax.ppermute only.
A program may use at most 64 MiB of HBM per device.

v0:
```python
import jax
import jax.numpy as jnp
from jax import lax
from jax.sharding import PartitionSpec as P

TOP = 8


def passed_along(value, axis, steps):
    count = lax.axis_size(axis)
    pairs = [(source, (source + steps) % count) for source in range(count)]
    return lax.ppermute(value, axis, pairs)


def body(
    layer_in, grad_out, gate_prob, expert_ids, replica_index, slot_expert, w_gate, w_up, w_down
):
    slots = lax.axis_size("expert")
    maxrep = min(4, slots // 8)
    tok_count = layer_in.shape[0]
    capacity = tok_count // maxrep
    recv_rows = slots * capacity
    expert_count = (8 - maxrep) * slots // 8
    slot_index = jnp.arange(slots, dtype=jnp.int32)
    expert_index = jnp.arange(expert_count, dtype=jnp.int32)
    is_start = slot_expert != jnp.roll(slot_expert, 1)
    first_slot = jnp.sum(
        jnp.where(
            (slot_expert[None, :] == expert_index[:, None]) & is_start[None, :],
            slot_index[None, :],
            0,
        ),
        axis=1,
    )
    expert_flat = expert_ids.reshape(-1)
    route_slot = jnp.sum(
        jnp.where(expert_flat[:, None] == expert_index[None, :], first_slot[None, :], 0), axis=1
    )
    route_slot = (route_slot + replica_index.reshape(-1)) % slots
    onehot = (route_slot[:, None] == slot_index[None, :]).astype(jnp.int32)
    rank_in_slot = jnp.sum((jnp.cumsum(onehot, axis=0) - onehot) * onehot, axis=1)
    position = route_slot * capacity + rank_in_slot
    prob_flat = gate_prob.reshape(-1)

    def pack(values):
        buffer = jnp.zeros((recv_rows, values.shape[1]), values.dtype).at[position].set(values)
        return buffer.reshape(slots, capacity, values.shape[1])

    repeated = jnp.repeat(grad_out, TOP, axis=0).astype(jnp.float32)
    inputs, scaled = (
        lax.all_gather(
            lax.all_to_all(
                pack(jnp.repeat(layer_in, TOP, axis=0)),
                "expert",
                split_axis=0,
                concat_axis=0,
                tiled=True,
            ),
            "dp",
            axis=2,
            tiled=True,
        ),
        lax.all_gather(
            lax.all_to_all(
                pack((prob_flat[:, None] * repeated).astype(jnp.bfloat16)),
                "expert",
                split_axis=0,
                concat_axis=0,
                tiled=True,
            ),
            "dp",
            axis=2,
            tiled=True,
        ),
    )
    inputs = inputs.reshape(recv_rows, -1)
    scaled = scaled.reshape(recv_rows, -1)
    width = inputs.shape[1]
    gate_matrix = w_gate[0]
    up_matrix = w_up[0]
    down_matrix = w_down[0]
    gate_pre = jnp.dot(inputs, gate_matrix, preferred_element_type=jnp.float32)
    up_pre = jnp.dot(inputs, up_matrix, preferred_element_type=jnp.float32)
    hidden = (jax.nn.silu(gate_pre) * up_pre).astype(jnp.bfloat16)
    slot_partial = lax.dot_general(
        hidden, scaled, (((0,), (0,)), ((), ())), preferred_element_type=jnp.float32
    ).astype(jnp.bfloat16)
    slot_partial, scaled = lax.optimization_barrier((slot_partial, scaled))
    contract_last = (((1,), (1,)), ((), ()))
    hidden_grad = lax.dot_general(
        scaled, down_matrix, contract_last, preferred_element_type=jnp.float32
    )
    sigma = jax.nn.sigmoid(gate_pre)
    gate_grad = (hidden_grad * up_pre * sigma * (1.0 + gate_pre * (1.0 - sigma))).astype(
        jnp.bfloat16
    )
    up_grad = (hidden_grad * gate_pre * sigma).astype(jnp.bfloat16)
    partial_value = lax.dot_general(
        gate_grad, gate_matrix, contract_last, preferred_element_type=jnp.float32
    )
    partial_value = partial_value + lax.dot_general(
        up_grad, up_matrix, contract_last, preferred_element_type=jnp.float32
    )
    partial_value = partial_value.reshape(slots, capacity, width)
    summed = lax.psum_scatter(
        partial_value.astype(jnp.bfloat16), "dp", scatter_dimension=2, tiled=True
    ).astype(jnp.float32)
    returned = lax.all_to_all(
        summed.astype(jnp.bfloat16), "expert", split_axis=0, concat_axis=0, tiled=True
    ).astype(summed.dtype)
    flat_back = returned.reshape(recv_rows, -1)
    grad_in = jnp.sum(flat_back[position].reshape(tok_count, TOP, -1), axis=1).astype(jnp.bfloat16)
    own_index = lax.axis_index("expert")
    expert_here = jnp.sum(jnp.where(slot_index == own_index, slot_expert, 0))

    def same_at(offset):
        neighbour = (own_index - offset) % slots
        match = jnp.any((slot_index == neighbour) & (slot_expert == expert_here))
        return match.astype(jnp.float32)

    own = slot_partial.astype(jnp.float32)
    left = own + same_at(1) * passed_along(slot_partial, "expert", 1).astype(jnp.float32)
    right = own + same_at(-1) * passed_along(slot_partial, "expert", -1).astype(jnp.float32)
    far_left = passed_along(left.astype(jnp.bfloat16), "expert", 2).astype(jnp.float32)
    far_right = passed_along(right.astype(jnp.bfloat16), "expert", -2).astype(jnp.float32)
    total = left + same_at(2) * far_left + (right - own) + same_at(-2) * far_right
    grad_w_down = total.astype(jnp.bfloat16)[None]
    return (grad_in, grad_w_down)


def solution(mesh):
    placed = (
        P("expert", "dp"),
        P("expert", "dp"),
        P("expert", None),
        P("expert", None),
        P("expert", None),
        P(),
        P("expert", None, "dp"),
        P("expert", None, "dp"),
        P("expert", "dp", None),
    )
    return jax.shard_map(
        body,
        mesh=mesh,
        in_specs=placed,
        out_specs=(P("expert", "dp"), P("expert", "dp", None)),
        check_vma=False,
    )
```

profile of v0, /device:TPU:6, one launch (start us, length us, event | category | flops | bytes accessed | tf_op | source)
XLA Modules:
  0.0 280.3 jit_solution(15586533807323691807)
XLA Ops:
  7.2 0.0 copy-start
  7.2 0.0 copy-start.6
  7.2 0.0 copy-start.7
  7.2 0.0 all-gather.3.cloned.1.call-start
  7.2 0.8 copy.18
  8.1 0.1 reshape.135
  8.2 0.1 reshape.134
  8.3 0.1 reshape.133
  8.4 1.2 slice.14
  9.6 1.3 fusion.41
  10.9 2.1 broadcast_compare_fusion
  13.0 0.8 select_reduce_fusion.1
  13.8 0.8 copy.17
  14.5 0.1 eq.98
  14.6 0.1 select_reduce_fusion
  14.7 0.6 reduce-window.6
  15.4 0.2 slice_reduce_fusion
  15.6 0.1 fusion.33
  15.7 1.9 scatter_custom_fusion
  17.6 50.4 %all_to_all.15 = bf16[64,8,512]{2,1,0:T(8,128)(2,1)} all-to-all(bf16[64,8,512]{2,1,0:T(8,128)(2,1)S(1)} %bitcast.69), channel_id=1, replica_groups=mesh['dp'=8,'expert'=64] {'expert'}, dimensions={0} | all-to-all | bytes 1048576 | tf_op jit(solution)/shard_map/all_to_all | solution.py:52
  68.0 0.0 all-gather.3.cloned.1.call-update
  68.0 0.0 all-gather.5.cloned.1.call-start
  68.1 0.0 copy-done.6
  68.1 0.0 copy-done.7
  68.1 0.1 copy.22
  68.2 0.1 mul.80
  68.3 1.7 scatter_custom_fusion.1
  70.0 37.4 %all_to_all.16 = bf16[64,8,512]{2,1,0:T(8,128)(2,1)} all-to-all(bf16[64,8,512]{2,1,0:T(8,128)(2,1)S(1)} %bitcast.70), channel_id=1, replica_groups=mesh['dp'=8,'expert'=64] {'expert'}, dimensions={0} | all-to-all | bytes 1048576 | tf_op jit(solution)/shard_map/all_to_all | solution.py:64
  107.4 0.0 all-gather.5.cloned.1.call-update
  107.4 0.0 copy-start.3
  107.4 0.0 reduce-scatter.2.cloned.1.call-start
  107.4 0.0 all-gather.3.cloned.1.call-done
  107.5 0.0 copy-done
  107.5 0.0 copy-start.1
  107.5 3.6 %fusion.3 = f32[512,128]{1,0:T(8,128)S(1)} fusion(bf16[64,8,4096]{2,1,0:T(8,128)(2,1)} %all-gather.3.cloned.1.call-done, bf16[1,4096,128]{2,1,0:T(8,128)(2,1)S(1)} %copy-done), kind=kOutput, calls=%fused_computation.8 | convolution fusion | flops 536870912 | bytes 5505024 | tf_op jit(solution)/shard_map/dot_general | solution.py:82
  111.1 0.0 copy-done.3
  111.1 0.1 copy-done.1
  111.2 2.0 fusion.1
  113.1 29.3 %all-gather.5.cloned.1.call-done = bf16[64,8,4096]{2,1,0:T(8,128)(2,1)} async-done(((bf16[64,8,512]{2,1,0:T(8,128)(2,1)}), bf16[64,8,4096]{2,1,0:T(8,128)(2,1)}) %all-gather.5.cloned.1.call-update) | async-done | bytes 4194320 | tf_op jit(solution)/shard_map/all_gather | solution.py:63
  142.5 3.2 %convolution_convert_fusion = bf16[128,4096]{1,0:T(8,128)(2,1)S(1)} fusion(f32[512,128]{1,0:T(8,128)} %fusion.1, f32[512,128]{1,0:T(8,128)S(1)} %fusion.3, bf16[64,8,4096]{2,1,0:T(8,128)(2,1)} %all-gather.5.cloned.1.call-done), kind=kOutput, calls=%fused_computation.5 | convolution fusion | flops 537788416 | bytes 5767168 | tf_op jit(solution)/shard_map/dot_general | solution.py:85
  145.7 0.3 copy-done.2
  146.0 0.3 copy-done.5
  146.3 1.2 fusion.10
  147.6 0.0 copy-done.4
  147.6 1.3 fusion.14
  148.8 3.2 %fusion = bf16[64,8,4096]{2,1,0:T(8,128)(2,1)} fusion(f32[512,4096]{1,0:T(8,128)S(1)} %fusion.14, bf16[1,4096,128]{2,1,0:T(8,128)(2,1)S(1)} %copy-done.3, f32[512,128]{1,0:T(8,128)S(1)} %fusion.10, f32[512,128]{1,0:T(8,128)S(1)} %fusion.3), kind=kOutput, calls=%fused_computation.4 | convolution fusion | flops 541458432 | bytes 14155776 | tf_op jit(solution)/shard_map/dot_general | solution.py:101
  152.0 0.0 reduce-scatter.2.cloned.1.call-update
  152.1 3.6 %collective-permute-start = (bf16[128,4096]{1,0:T(8,128)(2,1)S(1)}, bf16[128,4096]{1,0:T(8,128)(2,1)S(1)}, u32[]{:S(2)}, u32[]{:S(2)}) collective-permute-start(bf16[128,4096]{1,0:T(8,128)(2,1)S(1)} %convolution_convert_fusion), channel_id=1, source_target_pairs={{0,1},{1,2},{2,3},{3,4},{4,5},{5,6},{6,7},{7,8},{8,9},{9,10},{10,1... | collective-permute-start | bytes 3145736 | tf_op jit(solution)/shard_map/ppermute | solution.py:12
  155.7 4.7 %collective-permute-start.2 = (bf16[128,4096]{1,0:T(8,128)(2,1)S(1)}, bf16[128,4096]{1,0:T(8,128)(2,1)}, u32[]{:S(2)}, u32[]{:S(2)}) collective-permute-start(bf16[128,4096]{1,0:T(8,128)(2,1)S(1)} %convolution_convert_fusion), channel_id=1, source_target_pairs={{0,63},{1,0},{2,1},{3,2},{4,3},{5,4},{6,5},{7,6},{8,7},{9,8},{10,9... | collective-permute-start | bytes 3145736 | tf_op jit(solution)/shard_map/ppermute | solution.py:12
  160.5 0.7 and_reduce_fusion.2
  162.5 19.4 %collective-permute-done = bf16[128,4096]{1,0:T(8,128)(2,1)S(1)} collective-permute-done((bf16[128,4096]{1,0:T(8,128)(2,1)S(1)}, bf16[128,4096]{1,0:T(8,128)(2,1)S(1)}, u32[]{:S(2)}, u32[]{:S(2)}) %collective-permute-start) | collective-permute-done | bytes 1048608 | tf_op jit(solution)/shard_map/ppermute | solution.py:12
  181.9 1.4 collective-permute-done.2
  183.2 3.2 %fusion.9 = (bf16[128,4096]{1,0:T(8,128)(2,1)}, bf16[128,4096]{1,0:T(8,128)(2,1)}) fusion(bf16[128,4096]{1,0:T(8,128)(2,1)S(1)} %collective-permute-done, bf16[128,4096]{1,0:T(8,128)(2,1)S(1)} %convolution_convert_fusion, f32[]{:T(128)S(6)} %convert_element_type.90, bf16[128,4096]{1,0:T(8,128)(2,1)} %collective-permute-done.2, f32[]{:T(128)S(6)} %convert_element_type.95), kind=kLoop, calls=%fused_computation.17 | loop fusion | flops 4718592 | bytes 5242888 | tf_op jit(solution)/shard_map/convert_element_type | solution.py:124
  186.4 5.0 %collective-permute-start.1 = (bf16[128,4096]{1,0:T(8,128)(2,1)}, bf16[128,4096]{1,0:T(8,128)(2,1)}, u32[]{:S(2)}, u32[]{:S(2)}) collective-permute-start(bf16[128,4096]{1,0:T(8,128)(2,1)} %get-tuple-element.10), channel_id=1, source_target_pairs={{0,2},{1,3},{2,4},{3,5},{4,6},{5,7},{6,8},{7,9},{8,10},{9,11},{10,... | collective-permute-start | bytes 3145736 | tf_op jit(solution)/shard_map/ppermute | solution.py:12
  191.4 3.9 %collective-permute-start.3 = (bf16[128,4096]{1,0:T(8,128)(2,1)}, bf16[128,4096]{1,0:T(8,128)(2,1)}, u32[]{:S(2)}, u32[]{:S(2)}) collective-permute-start(bf16[128,4096]{1,0:T(8,128)(2,1)} %get-tuple-element.11), channel_id=1, source_target_pairs={{0,62},{1,63},{2,0},{3,1},{4,2},{5,3},{6,4},{7,5},{8,6},{9,7},{10,... | collective-permute-start | bytes 3145736 | tf_op jit(solution)/shard_map/ppermute | solution.py:12
  195.3 2.9 %reduce-scatter.2.cloned.1.call-done = bf16[64,8,512]{2,1,0:T(8,128)(2,1)} async-done(((bf16[64,8,4096]{2,1,0:T(8,128)(2,1)}), bf16[64,8,512]{2,1,0:T(8,128)(2,1)}) %reduce-scatter.2.cloned.1.call-update) | async-done | bytes 524304 | tf_op jit(solution)/shard_map/reduce_scatter | solution.py:105
  198.1 16.4 %all-to-all-start.2 = ((bf16[64,8,512]{2,1,0:T(8,128)(2,1)}), bf16[64,8,512]{2,1,0:T(8,128)(2,1)}, u32[]{:S(2)}, u32[]{:S(2)}) async-start(bf16[64,8,512]{2,1,0:T(8,128)(2,1)} %reduce-scatter.2.cloned.1.call-done), calls=%async_computation.3 | async-start | bytes 1048576 | tf_op jit(solution)/shard_map/all_to_all | solution.py:108
  215.9 7.9 %collective-permute-done.1 = bf16[128,4096]{1,0:T(8,128)(2,1)} collective-permute-done((bf16[128,4096]{1,0:T(8,128)(2,1)}, bf16[128,4096]{1,0:T(8,128)(2,1)}, u32[]{:S(2)}, u32[]{:S(2)}) %collective-permute-start.1) | collective-permute-done | bytes 1048608 | tf_op jit(solution)/shard_map/ppermute | solution.py:12
  223.8 22.4 %collective-permute-done.3 = bf16[128,4096]{1,0:T(8,128)(2,1)} collective-permute-done((bf16[128,4096]{1,0:T(8,128)(2,1)}, bf16[128,4096]{1,0:T(8,128)(2,1)}, u32[]{:S(2)}, u32[]{:S(2)}) %collective-permute-start.3) | collective-permute-done | bytes 1048608 | tf_op jit(solution)/shard_map/ppermute | solution.py:12
  246.2 3.9 %fusion.17 = bf16[1,128,4096]{2,1,0:T(8,128)(2,1)} fusion(bf16[128,4096]{1,0:T(8,128)(2,1)} %collective-permute-done.3, f32[]{:T(128)S(6)} %convert_element_type.97, bf16[128,4096]{1,0:T(8,128)(2,1)} %collective-permute-done.2, f32[]{:T(128)S(6)} %convert_element_type.95, bf16[128,4096]{1,0:T(8,128)(2,1)} %collective-permute-done.1, ...), kind=kLoop, calls=%fused_computation.25 | loop fusion | flops 8388608 | bytes 6291472 | tf_op jit(solution)/shard_map/broadcast_in_dim | solution.py:127
  250.1 20.8 %all-to-all-done.2 = bf16[64,8,512]{2,1,0:T(8,128)(2,1)} async-done(((bf16[64,8,512]{2,1,0:T(8,128)(2,1)}), bf16[64,8,512]{2,1,0:T(8,128)(2,1)}, u32[]{:S(2)}, u32[]{:S(2)}) %all-to-all-start.2) | async-done | bytes 524320 | tf_op jit(solution)/shard_map/all_to_all | solution.py:108
  270.9 1.2 bitcast_convert_fusion
  272.1 1.0 gather_fusion
  273.0 0.7 bitcast_reduce_fusion
  (11 shorter events, 0.1 us)
Async XLA Ops:
  7.2 100.3 %copy-start = (bf16[1,4096,128]{2,1,0:T(8,128)(2,1)S(1)}, bf16[1,4096,128]{2,1,0:T(8,128)(2,1)}, u32[]{:S(2)}) copy-start(bf16[1,4096,128]{2,1,0:T(8,128)(2,1)} %param.15) | copy-start | bytes 3145732
  7.2 60.9 %copy-start.6 = (bf16[32,512]{1,0:T(8,128)(2,1)S(1)}, bf16[32,512]{1,0:T(8,128)(2,1)}, u32[]{:S(2)}) copy-start(bf16[32,512]{1,0:T(8,128)(2,1)} %param.10) | copy-start | bytes 98308
  7.2 60.9 %copy-start.7 = (f32[32,8]{0,1:T(8,128)S(1)}, f32[32,8]{0,1:T(8,128)}, u32[]{:S(2)}) copy-start(f32[32,8]{0,1:T(8,128)} %param.11) | copy-start | bytes 3076
  7.2 100.3 %all-gather.3.cloned.1.call-start = ((), (), s32[]{:S(2)}) async-start(), calls=%async_computation.4 | async-start | bytes 4718592 | tf_op jit(solution)/shard_map/all_gather | solution.py:51
  68.0 74.5 %all-gather.5.cloned.1.call-start = ((), (), s32[]{:S(2)}) async-start(), calls=%async_computation.5 | async-start | bytes 4718592 | tf_op jit(solution)/shard_map/all_gather | solution.py:63
  107.4 3.7 %copy-start.3 = (bf16[1,4096,128]{2,1,0:T(8,128)(2,1)S(1)}, bf16[1,4096,128]{2,1,0:T(8,128)(2,1)}, u32[]{:S(2)}) copy-start(bf16[1,4096,128]{2,1,0:T(8,128)(2,1)} %param.16) | copy-start | bytes 3145732
  107.4 90.7 %reduce-scatter.2.cloned.1.call-start = ((), (), s32[]{:S(2)}) async-start(), calls=%async_computation.6 | async-start | bytes 4718592 | tf_op jit(solution)/shard_map/reduce_scatter | solution.py:105
  107.5 3.7 %copy-start.1 = (bf16[64,8,4096]{2,1,0:T(8,128)(2,1)S(1)}, bf16[64,8,4096]{2,1,0:T(8,128)(2,1)}, u32[]{:S(2)}) copy-start(bf16[64,8,4096]{2,1,0:T(8,128)(2,1)} %all-gather.3.cloned.1.call-done) | copy-start | bytes 12582916
  142.5 3.5 %copy-start.2 = (bf16[64,8,4096]{2,1,0:T(8,128)(2,1)S(1)}, bf16[64,8,4096]{2,1,0:T(8,128)(2,1)}, u32[]{:S(2)}) copy-start(bf16[64,8,4096]{2,1,0:T(8,128)(2,1)} %all-gather.5.cloned.1.call-done) | copy-start | bytes 12582916
  142.5 3.8 %copy-start.5 = (bf16[1,128,4096]{2,1,0:T(8,128)(2,1)S(1)}, bf16[1,128,4096]{2,1,0:T(8,128)(2,1)}, u32[]{:S(2)}) copy-start(bf16[1,128,4096]{2,1,0:T(8,128)(2,1)} %param.17) | copy-start | bytes 3145732
  146.3 1.3 copy-start.4
  152.1 29.8 %collective-permute-start = (bf16[128,4096]{1,0:T(8,128)(2,1)S(1)}, bf16[128,4096]{1,0:T(8,128)(2,1)S(1)}, u32[]{:S(2)}, u32[]{:S(2)}) collective-permute-start(bf16[128,4096]{1,0:T(8,128)(2,1)S(1)} %convolution_convert_fusion), channel_id=1, source_target_pairs={{0,1},{1,2},{2,3},{3,4},{4,5},{5,6},{6,7},{7,8},{8,9},{9,10},{10,1... | collective-permute-start | bytes 3145736 | tf_op jit(solution)/shard_map/ppermute | solution.py:12
  155.7 27.5 %collective-permute-start.2 = (bf16[128,4096]{1,0:T(8,128)(2,1)S(1)}, bf16[128,4096]{1,0:T(8,128)(2,1)}, u32[]{:S(2)}, u32[]{:S(2)}) collective-permute-start(bf16[128,4096]{1,0:T(8,128)(2,1)S(1)} %convolution_convert_fusion), channel_id=1, source_target_pairs={{0,63},{1,0},{2,1},{3,2},{4,3},{5,4},{6,5},{7,6},{8,7},{9,8},{10,9... | collective-permute-start | bytes 3145736 | tf_op jit(solution)/shard_map/ppermute | solution.py:12
  186.4 37.4 %collective-permute-start.1 = (bf16[128,4096]{1,0:T(8,128)(2,1)}, bf16[128,4096]{1,0:T(8,128)(2,1)}, u32[]{:S(2)}, u32[]{:S(2)}) collective-permute-start(bf16[128,4096]{1,0:T(8,128)(2,1)} %get-tuple-element.10), channel_id=1, source_target_pairs={{0,2},{1,3},{2,4},{3,5},{4,6},{5,7},{6,8},{7,9},{8,10},{9,11},{10,... | collective-permute-start | bytes 3145736 | tf_op jit(solution)/shard_map/ppermute | solution.py:12
  191.4 54.8 %collective-permute-start.3 = (bf16[128,4096]{1,0:T(8,128)(2,1)}, bf16[128,4096]{1,0:T(8,128)(2,1)}, u32[]{:S(2)}, u32[]{:S(2)}) collective-permute-start(bf16[128,4096]{1,0:T(8,128)(2,1)} %get-tuple-element.11), channel_id=1, source_target_pairs={{0,62},{1,63},{2,0},{3,1},{4,2},{5,3},{6,4},{7,5},{8,6},{9,7},{10,... | collective-permute-start | bytes 3145736 | tf_op jit(solution)/shard_map/ppermute | solution.py:12
  198.1 72.8 %all-to-all-start.2 = ((bf16[64,8,512]{2,1,0:T(8,128)(2,1)}), bf16[64,8,512]{2,1,0:T(8,128)(2,1)}, u32[]{:S(2)}, u32[]{:S(2)}) async-start(bf16[64,8,512]{2,1,0:T(8,128)(2,1)} %reduce-scatter.2.cloned.1.call-done), calls=%async_computation.3 | async-start | bytes 1048576 | tf_op jit(solution)/shard_map/all_to_all | solution.py:108
Sparse Core Ops, SparseCore 0:
  68.1 32.3 all-gather.2
  107.5 34.9 all-gather.4
  152.2 45.9 reduce-scatter.1
where the time goes:
time: 281 us; the launch traced here: 280 us
  waiting for transfers between devices  104 us (37%)
  blocking collectives  87.7 us (31%)
  starting transfers between devices  33.7 us (12%)
  between operations  16.6 us (6%)
  other arithmetic  16.5 us (6%)
  matrix products  14.5 us (5%)
  local copies, waits for them, and re-layouts  7.14 us (3%)
    ppermute x4, waiting for transfers between devices, passed_along(): return lax.ppermute(value, axis, pairs)  51.1 us
    all_to_all x1, blocking collectives, body(): lax.all_to_all(pack(jnp.repeat(layer_in, TOP, axis=0)), 'expert', split_a...  50.4 us
    all_to_all x1, blocking collectives, body(): lax.all_to_all(pack((prob_flat[:, None] * repeated).astype(jnp.bfloat16))...  37.4 us
    all_gather x1, waiting for transfers between devices, body(): lax.all_gather(lax.all_to_all(pack((prob_flat[:, None] * repeated).astype...  29.3 us
    all_to_all x1, waiting for transfers between devices, body(): lax.all_to_all(summed.astype(jnp.bfloat16), 'expert', split_axis=0, conca...  20.8 us
    ppermute x4, starting transfers between devices, passed_along(): return lax.ppermute(value, axis, pairs)  17.2 us
    all_to_all x1, starting transfers between devices, body(): lax.all_to_all(summed.astype(jnp.bfloat16), 'expert', split_axis=0, conca...  16.4 us
  transfers between devices with their start and end apart: 8, of which 7 were waited for; matrix products, arithmetic and copies ran while one was open for 5% of the time, Pallas kernels for 0%

commit v1 on v0

--- a/solution.py
+++ b/solution.py
@@ -60,17 +60,25 @@
             axis=2,
             tiled=True,
         ),
-        lax.all_gather(
-            lax.all_to_all(
-                pack((prob_flat[:, None] * repeated).astype(jnp.bfloat16)),
-                "expert",
+        jnp.concatenate(
+            jax.lax.all_to_all(
+                jnp.stack(
+                    [
+                        lax.all_to_all(
+                            pack((prob_flat[:, None] * repeated).astype(jnp.bfloat16)),
+                            "expert",
+                            split_axis=0,
+                            concat_axis=0,
+                            tiled=True,
+                        )
+                    ]
+                    * jax.lax.psum(1, axis_name="dp")
+                ),
+                axis_name="dp",
                 split_axis=0,
                 concat_axis=0,
-                tiled=True,
             ),
-            "dp",
             axis=2,
-            tiled=True,
         ),
     )
     inputs = inputs.reshape(recv_rows, -1)

time: 281 us -> 304 us (1.082)
  blocking collectives: 87.7 us -> 142 us
  waiting for transfers between devices: 104 us -> 69.6 us
  local copies, waits for them, and re-layouts: 7.14 us -> 17 us
  starting transfers between devices: 33.7 us -> 28.3 us
    all_to_all x0 -> x1, blocking collectives: none -> 54.6 us  [body(): jax.lax.all_to_all(jnp.stack([lax.all_to_all(pack((prob_flat[:, None] * r...]
    all_gather x1 -> x0, waiting for transfers between devices: 29.3 us -> none  [body(): lax.all_gather(lax.all_to_all(pack((prob_flat[:, None] * repeated).astype...]
    all_to_all x1, waiting for transfers between devices: 20.8 us -> 5.28 us  [body(): lax.all_to_all(summed.astype(jnp.bfloat16), 'expert', split_axis=0, conca...]
    ppermute x4, waiting for transfers between devices: 51.1 us -> 64.3 us  [passed_along(): return lax.ppermute(value, axis, pairs)]
    unnamed x19 -> x18, local copies, waits for them, and re-layouts: 2.42 us -> 7.43 us
    all_to_all x1, starting transfers between devices: 16.4 us -> 11.5 us  [body(): lax.all_to_all(summed.astype(jnp.bfloat16), 'expert', split_axis=0, conca...]
    reshape x0 -> x1, local copies, waits for them, and re-layouts: none -> 4.54 us  [body(): jnp.concatenate(jax.lax.all_to_all(jnp.stack([lax.all_to_all(pack((prob_f...]
  transfers between devices with their start and end apart: 8 -> 7, of which waited for: 7 -> 5; matrix products, arithmetic and copies ran while one was open for 5% -> 6% of each run, Pallas kernels for 0% -> 0%
where the time goes in v1:
time: 304 us; the launch traced here: 302 us
  blocking collectives  142 us (47%)
  waiting for transfers between devices  69.6 us (23%)
  starting transfers between devices  28.3 us (9%)
  local copies, waits for them, and re-layouts  17 us (6%)
  between operations  16.9 us (6%)
  other arithmetic  16.5 us (5%)
  matrix products  11.6 us (4%)
    ppermute x4, waiting for transfers between devices, passed_along(): return lax.ppermute(value, axis, pairs)  64.3 us
    all_to_all x1, blocking collectives, body(): jax.lax.all_to_all(jnp.stack([lax.all_to_all(pack((prob_flat[:, None] * r...  54.6 us
    all_to_all x1, blocking collectives, body(): lax.all_to_all(pack(jnp.repeat(layer_in, TOP, axis=0)), 'expert', split_a...  50.4 us
    all_to_all x1, blocking collectives, body(): lax.all_to_all(pack((prob_flat[:, None] * repeated).astype(jnp.bfloat16))...  37.3 us
    ppermute x4, starting transfers between devices, passed_along(): return lax.ppermute(value, axis, pairs)  16.8 us
    all_to_all x1, starting transfers between devices, body(): lax.all_to_all(summed.astype(jnp.bfloat16), 'expert', split_axis=0, conca...  11.5 us
    unnamed x18, local copies, waits for them, and re-layouts  7.43 us
  transfers between devices with their start and end apart: 7, of which 5 were waited for; matrix products, arithmetic and copies ran while one was open for 6% of the time, Pallas kernels for 0%

profile of v1, /device:TPU:6, one launch (start us, length us, event | category | flops | bytes accessed | tf_op | source)
XLA Modules:
  0.0 302.2 jit_solution(5225871049071796500)
XLA Ops:
  7.2 0.0 copy-start
  7.2 0.0 copy-start.5
  7.2 0.0 copy-start.6
  7.2 0.0 all-gather.2.cloned.1.call-start
  7.2 0.8 copy.25
  8.1 0.1 reshape.137
  8.2 0.1 reshape.136
  8.3 0.1 reshape.135
  8.4 1.2 slice.14
  9.6 1.3 fusion.41
  10.9 2.1 broadcast_compare_fusion
  13.0 0.8 select_reduce_fusion.1
  13.8 0.8 copy.24
  14.5 0.1 eq.98
  14.6 0.1 select_reduce_fusion
  14.7 0.6 reduce-window.6
  15.4 0.2 slice_reduce_fusion
  15.6 0.1 fusion.33
  15.7 1.9 scatter_custom_fusion
  17.6 50.4 %all_to_all.20 = bf16[64,8,512]{2,1,0:T(8,128)(2,1)} all-to-all(bf16[64,8,512]{2,1,0:T(8,128)(2,1)S(1)} %bitcast.75), channel_id=1, replica_groups=mesh['dp'=8,'expert'=64] {'expert'}, dimensions={0} | all-to-all | bytes 1048576 | tf_op jit(solution)/shard_map/all_to_all | solution.py:52
  68.0 0.0 all-gather.2.cloned.1.call-update
  68.0 0.0 reduce-scatter.2.cloned.1.call-start
  68.1 0.0 copy-done.5
  68.1 0.0 copy-done.6
  68.1 0.1 copy.29
  68.2 0.1 mul.80
  68.3 1.7 scatter_custom_fusion.1
  70.0 37.3 %all_to_all.21 = bf16[64,8,512]{2,1,0:T(8,128)(2,1)S(1)} all-to-all(bf16[64,8,512]{2,1,0:T(8,128)(2,1)S(1)} %bitcast.76), channel_id=1, replica_groups=mesh['dp'=8,'expert'=64] {'expert'}, dimensions={0} | all-to-all | bytes 1048576 | tf_op jit(solution)/shard_map/all_to_all | solution.py:67
  107.3 0.4 stack.2
  107.6 54.6 %all_to_all.22 = bf16[8,64,8,512]{3,2,1,0:T(8,128)(2,1)S(1)} all-to-all(bf16[8,64,8,512]{3,2,1,0:T(8,128)(2,1)S(1)} %stack.2), channel_id=1, replica_groups=mesh['dp'=8,'expert'=64] {'dp'}, dimensions={0} | all-to-all | bytes 8388608 | tf_op jit(solution)/shard_map/all_to_all | solution.py:64
  162.2 4.5 %copy.35 = bf16[64,8,8,512]{3,2,1,0:T(8,128)(2,1)S(1)} copy(bf16[64,8,8,512]{3,1,0,2:T(8,128)(2,1)S(1)} %bitcast.74) | data formatting | bytes 8388608 | tf_op jit(solution)/shard_map/reshape | solution.py:63
  166.8 4.2 %copy.32 = bf16[64,8,8,512]{3,1,2,0:T(8,128)(2,1)} copy(bf16[64,8,8,512]{3,2,1,0:T(8,128)(2,1)S(1)} %copy.35) | data formatting | bytes 8388608
  171.0 0.0 copy-start.3
  171.0 0.0 all-gather.2.cloned.1.call-done
  171.0 0.0 copy-done
  171.0 0.0 copy-start.2
  171.0 3.6 %fusion.3 = f32[512,128]{1,0:T(8,128)S(1)} fusion(bf16[64,8,4096]{2,1,0:T(8,128)(2,1)} %all-gather.2.cloned.1.call-done, bf16[1,4096,128]{2,1,0:T(8,128)(2,1)S(1)} %copy-done), kind=kOutput, calls=%fused_computation.8 | convolution fusion | flops 536870912 | bytes 5505024 | tf_op jit(solution)/shard_map/dot_general | solution.py:90
  174.6 0.0 copy-done.3
  174.6 0.2 copy-done.2
  174.7 1.3 fusion.1
  176.0 0.9 copy-done.1
  176.9 0.8 convolution_convert_fusion
  177.7 0.4 copy-done.4
  178.1 1.3 fusion.10
  179.4 1.5 fusion.14
  180.9 3.2 %fusion = bf16[64,8,4096]{2,1,0:T(8,128)(2,1)} fusion(f32[512,4096]{1,0:T(8,128)S(1)} %fusion.14, bf16[1,4096,128]{2,1,0:T(8,128)(2,1)S(1)} %copy-done.3, f32[512,128]{1,0:T(8,128)S(1)} %fusion.10, f32[512,128]{1,0:T(8,128)S(1)} %fusion.3), kind=kOutput, calls=%fused_computation.4 | convolution fusion | flops 541458432 | bytes 14155776 | tf_op jit(solution)/shard_map/dot_general | solution.py:109
  184.1 0.0 reduce-scatter.2.cloned.1.call-update
  184.2 3.3 %collective-permute-start = (bf16[128,4096]{1,0:T(8,128)(2,1)S(1)}, bf16[128,4096]{1,0:T(8,128)(2,1)S(1)}, u32[]{:S(2)}, u32[]{:S(2)}) collective-permute-start(bf16[128,4096]{1,0:T(8,128)(2,1)S(1)} %convolution_convert_fusion), channel_id=1, source_target_pairs={{0,1},{1,2},{2,3},{3,4},{4,5},{5,6},{6,7},{7,8},{8,9},{9,10},{10,1... | collective-permute-start | bytes 3145736 | tf_op jit(solution)/shard_map/ppermute | solution.py:12
  187.5 4.6 %collective-permute-start.2 = (bf16[128,4096]{1,0:T(8,128)(2,1)S(1)}, bf16[128,4096]{1,0:T(8,128)(2,1)}, u32[]{:S(2)}, u32[]{:S(2)}) collective-permute-start(bf16[128,4096]{1,0:T(8,128)(2,1)S(1)} %convolution_convert_fusion), channel_id=1, source_target_pairs={{0,63},{1,0},{2,1},{3,2},{4,3},{5,4},{6,5},{7,6},{8,7},{9,8},{10,9... | collective-permute-start | bytes 3145736 | tf_op jit(solution)/shard_map/ppermute | solution.py:12
  192.2 0.7 and_reduce_fusion.2
  194.2 18.5 %collective-permute-done = bf16[128,4096]{1,0:T(8,128)(2,1)S(1)} collective-permute-done((bf16[128,4096]{1,0:T(8,128)(2,1)S(1)}, bf16[128,4096]{1,0:T(8,128)(2,1)S(1)}, u32[]{:S(2)}, u32[]{:S(2)}) %collective-permute-start) | collective-permute-done | bytes 1048608 | tf_op jit(solution)/shard_map/ppermute | solution.py:12
  212.7 1.2 collective-permute-done.2
  213.9 3.2 %fusion.9 = (bf16[128,4096]{1,0:T(8,128)(2,1)}, bf16[128,4096]{1,0:T(8,128)(2,1)}) fusion(bf16[128,4096]{1,0:T(8,128)(2,1)S(1)} %collective-permute-done, bf16[128,4096]{1,0:T(8,128)(2,1)S(1)} %convolution_convert_fusion, f32[]{:T(128)S(6)} %convert_element_type.90, bf16[128,4096]{1,0:T(8,128)(2,1)} %collective-permute-done.2, f32[]{:T(128)S(6)} %convert_element_type.95), kind=kLoop, calls=%fused_computation.18 | loop fusion | flops 4718592 | bytes 5242888 | tf_op jit(solution)/shard_map/convert_element_type | solution.py:132
  217.1 2.7 collective-permute-start.1
  219.8 6.1 %collective-permute-start.3 = (bf16[128,4096]{1,0:T(8,128)(2,1)}, bf16[128,4096]{1,0:T(8,128)(2,1)}, u32[]{:S(2)}, u32[]{:S(2)}) collective-permute-start(bf16[128,4096]{1,0:T(8,128)(2,1)} %get-tuple-element.11), channel_id=1, source_target_pairs={{0,62},{1,63},{2,0},{3,1},{4,2},{5,3},{6,4},{7,5},{8,6},{9,7},{10,... | collective-permute-start | bytes 3145736 | tf_op jit(solution)/shard_map/ppermute | solution.py:12
  225.9 0.0 reduce-scatter.2.cloned.1.call-done
  226.0 11.5 %all-to-all-start.3 = ((bf16[64,8,512]{2,1,0:T(8,128)(2,1)}), bf16[64,8,512]{2,1,0:T(8,128)(2,1)}, u32[]{:S(2)}, u32[]{:S(2)}) async-start(bf16[64,8,512]{2,1,0:T(8,128)(2,1)} %reduce-scatter.2.cloned.1.call-done), calls=%async_computation.4 | async-start | bytes 1048576 | tf_op jit(solution)/shard_map/all_to_all | solution.py:116
  238.7 39.7 %collective-permute-done.1 = bf16[128,4096]{1,0:T(8,128)(2,1)} collective-permute-done((bf16[128,4096]{1,0:T(8,128)(2,1)}, bf16[128,4096]{1,0:T(8,128)(2,1)}, u32[]{:S(2)}, u32[]{:S(2)}) %collective-permute-start.1) | collective-permute-done | bytes 1048608 | tf_op jit(solution)/shard_map/ppermute | solution.py:12
  278.4 4.9 %collective-permute-done.3 = bf16[128,4096]{1,0:T(8,128)(2,1)} collective-permute-done((bf16[128,4096]{1,0:T(8,128)(2,1)}, bf16[128,4096]{1,0:T(8,128)(2,1)}, u32[]{:S(2)}, u32[]{:S(2)}) %collective-permute-start.3) | collective-permute-done | bytes 1048608 | tf_op jit(solution)/shard_map/ppermute | solution.py:12
  283.3 3.9 %fusion.17 = bf16[1,128,4096]{2,1,0:T(8,128)(2,1)} fusion(bf16[128,4096]{1,0:T(8,128)(2,1)} %collective-permute-done.3, f32[]{:T(128)S(6)} %convert_element_type.97, bf16[128,4096]{1,0:T(8,128)(2,1)} %collective-permute-done.2, f32[]{:T(128)S(6)} %convert_element_type.95, bf16[128,4096]{1,0:T(8,128)(2,1)} %collective-permute-done.1, ...), kind=kLoop, calls=%fused_computation.26 | loop fusion | flops 8388608 | bytes 6291472 | tf_op jit(solution)/shard_map/broadcast_in_dim | solution.py:135
  287.2 5.3 %all-to-all-done.3 = bf16[64,8,512]{2,1,0:T(8,128)(2,1)} async-done(((bf16[64,8,512]{2,1,0:T(8,128)(2,1)}), bf16[64,8,512]{2,1,0:T(8,128)(2,1)}, u32[]{:S(2)}, u32[]{:S(2)}) %all-to-all-start.3) | async-done | bytes 524320 | tf_op jit(solution)/shard_map/all_to_all | solution.py:116
  292.5 1.2 bitcast_convert_fusion
  293.7 1.0 gather_fusion
  294.6 0.7 bitcast_reduce_fusion
  (10 shorter events, 0.1 us)
Async XLA Ops:
  7.2 163.8 %copy-start = (bf16[1,4096,128]{2,1,0:T(8,128)(2,1)S(1)}, bf16[1,4096,128]{2,1,0:T(8,128)(2,1)}, u32[]{:S(2)}) copy-start(bf16[1,4096,128]{2,1,0:T(8,128)(2,1)} %param.15) | copy-start | bytes 3145732
  7.2 60.9 %copy-start.5 = (bf16[32,512]{1,0:T(8,128)(2,1)S(1)}, bf16[32,512]{1,0:T(8,128)(2,1)}, u32[]{:S(2)}) copy-start(bf16[32,512]{1,0:T(8,128)(2,1)} %param.10) | copy-start | bytes 98308
  7.2 60.9 %copy-start.6 = (f32[32,8]{0,1:T(8,128)S(1)}, f32[32,8]{0,1:T(8,128)}, u32[]{:S(2)}) copy-start(f32[32,8]{0,1:T(8,128)} %param.11) | copy-start | bytes 3076
  7.2 163.8 %all-gather.2.cloned.1.call-start = ((), (), s32[]{:S(2)}) async-start(), calls=%async_computation.5 | async-start | bytes 4718592 | tf_op jit(solution)/shard_map/all_gather | solution.py:51
  68.0 157.9 %reduce-scatter.2.cloned.1.call-start = ((), (), s32[]{:S(2)}) async-start(), calls=%async_computation.6 | async-start | bytes 4718592 | tf_op jit(solution)/shard_map/reduce_scatter | solution.py:113
  171.0 3.6 %copy-start.3 = (bf16[1,4096,128]{2,1,0:T(8,128)(2,1)S(1)}, bf16[1,4096,128]{2,1,0:T(8,128)(2,1)}, u32[]{:S(2)}) copy-start(bf16[1,4096,128]{2,1,0:T(8,128)(2,1)} %param.16) | copy-start | bytes 3145732
  171.0 3.8 %copy-start.2 = (bf16[64,8,4096]{2,1,0:T(8,128)(2,1)S(1)}, bf16[64,8,4096]{2,1,0:T(8,128)(2,1)}, u32[]{:S(2)}) copy-start(bf16[64,8,4096]{2,1,0:T(8,128)(2,1)} %all-gather.2.cloned.1.call-done) | copy-start | bytes 12582916
  174.7 2.2 copy-start.1
  176.9 1.2 copy-start.4
  184.2 28.5 %collective-permute-start = (bf16[128,4096]{1,0:T(8,128)(2,1)S(1)}, bf16[128,4096]{1,0:T(8,128)(2,1)S(1)}, u32[]{:S(2)}, u32[]{:S(2)}) collective-permute-start(bf16[128,4096]{1,0:T(8,128)(2,1)S(1)} %convolution_convert_fusion), channel_id=1, source_target_pairs={{0,1},{1,2},{2,3},{3,4},{4,5},{5,6},{6,7},{7,8},{8,9},{9,10},{10,1... | collective-permute-start | bytes 3145736 | tf_op jit(solution)/shard_map/ppermute | solution.py:12
  187.5 26.4 %collective-permute-start.2 = (bf16[128,4096]{1,0:T(8,128)(2,1)S(1)}, bf16[128,4096]{1,0:T(8,128)(2,1)}, u32[]{:S(2)}, u32[]{:S(2)}) collective-permute-start(bf16[128,4096]{1,0:T(8,128)(2,1)S(1)} %convolution_convert_fusion), channel_id=1, source_target_pairs={{0,63},{1,0},{2,1},{3,2},{4,3},{5,4},{6,5},{7,6},{8,7},{9,8},{10,9... | collective-permute-start | bytes 3145736 | tf_op jit(solution)/shard_map/ppermute | solution.py:12
  217.1 61.3 %collective-permute-start.1 = (bf16[128,4096]{1,0:T(8,128)(2,1)}, bf16[128,4096]{1,0:T(8,128)(2,1)}, u32[]{:S(2)}, u32[]{:S(2)}) collective-permute-start(bf16[128,4096]{1,0:T(8,128)(2,1)} %get-tuple-element.10), channel_id=1, source_target_pairs={{0,2},{1,3},{2,4},{3,5},{4,6},{5,7},{6,8},{7,9},{8,10},{9,11},{10,... | collective-permute-start | bytes 3145736 | tf_op jit(solution)/shard_map/ppermute | solution.py:12
  219.8 63.5 %collective-permute-start.3 = (bf16[128,4096]{1,0:T(8,128)(2,1)}, bf16[128,4096]{1,0:T(8,128)(2,1)}, u32[]{:S(2)}, u32[]{:S(2)}) collective-permute-start(bf16[128,4096]{1,0:T(8,128)(2,1)} %get-tuple-element.11), channel_id=1, source_target_pairs={{0,62},{1,63},{2,0},{3,1},{4,2},{5,3},{6,4},{7,5},{8,6},{9,7},{10,... | collective-permute-start | bytes 3145736 | tf_op jit(solution)/shard_map/ppermute | solution.py:12
  226.0 66.5 %all-to-all-start.3 = ((bf16[64,8,512]{2,1,0:T(8,128)(2,1)}), bf16[64,8,512]{2,1,0:T(8,128)(2,1)}, u32[]{:S(2)}, u32[]{:S(2)}) async-start(bf16[64,8,512]{2,1,0:T(8,128)(2,1)} %reduce-scatter.2.cloned.1.call-done), calls=%async_computation.4 | async-start | bytes 1048576 | tf_op jit(solution)/shard_map/all_to_all | solution.py:116
Sparse Core Ops, SparseCore 0:
  68.1 32.3 all-gather.1
  184.3 36.7 reduce-scatter.1
